TPU v7x, 32 devices: a whole 2x2x4 slice. The times are simulated.
32 devices in a mesh: energy: 16 (over z, y, x), space: 2 (over core).
Axes of the slice: x: 2, y: 2, z: 4, core: 2. Of those that a mesh axis runs over, the one named last changes fastest.
Arguments:
- lesser: bfloat16 [32, 2, 2, 256, 256], P('energy', 'space'), may hold values from -6 to 6
- greater: bfloat16 [32, 2, 2, 256, 256], P('energy', 'space'), may hold values from -6 to 6
- coulomb_diag: bfloat16 [2, 256, 256], P('space'), may hold values from -0.375 to 0.375
- coulomb_upper: bfloat16 [2, 256, 256], P('space'), may hold values from -0.375 to 0.375
Outputs:
- screened: bfloat16 [32, 2, 2, 256, 256], P('energy', 'space')
All inputs are finite; a program needn't handle non-finite values.
Results may differ from a plain program's by a relative error of at most 0.015.
Values may be sent and summed in bfloat16 or wider, within the bound.
A program may use at most 64 MiB of HBM per device.

v0:
```python
import math
import jax
import jax.numpy as jnp
from jax import lax
from jax.sharding import PartitionSpec as P


def from_behind(value, axis, steps):
    count = lax.axis_size(axis)
    leading, last = (max(0, -steps), min(count, count - steps))
    return lax.ppermute(value, axis, [(source, source + steps) for source in range(leading, last)])


def split_parts(values):
    high = values.astype(jnp.bfloat16)
    low = (values - high.astype(jnp.float32)).astype(jnp.bfloat16)
    return (high, low)


def product_two(table, data_bf):
    return jnp.dot(table[0], data_bf, preferred_element_type=jnp.float32) + jnp.dot(
        table[1], data_bf, preferred_element_type=jnp.float32
    )


def product_three(table, data_f32):
    data_high, data_low = split_parts(data_f32)
    total = jnp.dot(table[0], data_high, preferred_element_type=jnp.float32)
    total = total + jnp.dot(table[1], data_high, preferred_element_type=jnp.float32)
    return total + jnp.dot(table[0], data_low, preferred_element_type=jnp.float32)


def correlate(lesser_x, greater_x):
    energies = lesser_x.shape[0]
    length = 2 * energies
    tail_shape = lesser_x.shape[1:]

    def flatten(values, part):
        return values[:, :, part].reshape(energies, -1)

    lesser_re = flatten(lesser_x, 0)
    lesser_im = flatten(lesser_x, 1)
    greater_re = flatten(greater_x, 0)
    greater_im = flatten(greater_x, 1)
    freqs = lax.broadcasted_iota(jnp.int32, (length, energies), 0)
    places = lax.broadcasted_iota(jnp.int32, (length, energies), 1)
    angles = 2.0 * math.pi / length * jnp.mod(freqs * places, length).astype(jnp.float32)
    cosine = split_parts(jnp.cos(angles))
    sine = split_parts(jnp.sin(angles))
    cosine_t = split_parts(jnp.cos(angles).T)
    sine_t = split_parts(jnp.sin(angles).T)
    hat_lre = product_two(cosine, lesser_re) + product_two(sine, lesser_im)
    hat_lim = product_two(cosine, lesser_im) - product_two(sine, lesser_re)
    hat_gre = product_two(cosine, greater_re) - product_two(sine, greater_im)
    hat_gim = product_two(cosine, greater_im) + product_two(sine, greater_re)
    prod_re = hat_lre * hat_gre - hat_lim * hat_gim
    prod_im = hat_lre * hat_gim + hat_lim * hat_gre
    corr_re = (product_three(cosine_t, prod_re) - product_three(sine_t, prod_im)) / length
    corr_im = (product_three(cosine_t, prod_im) + product_three(sine_t, prod_re)) / length
    factor = jnp.float32(energies) ** (-0.5)
    shaped = (energies, tail_shape[0], tail_shape[2], tail_shape[3])
    real_part = (corr_im * factor).reshape(shaped)
    imag_part = (-corr_re * factor).reshape(shaped)
    return jnp.stack([real_part, imag_part], axis=2).astype(jnp.bfloat16)


def left_plain(coupler, blocks):
    return jnp.einsum("ab,ecbd->ecad", coupler, blocks, preferred_element_type=jnp.float32).astype(
        jnp.bfloat16
    )


def left_transposed(coupler, blocks):
    return jnp.einsum("ba,ecbd->ecad", coupler, blocks, preferred_element_type=jnp.float32).astype(
        jnp.bfloat16
    )


def right_transposed(left, coupler):
    return jnp.einsum("ecad,fd->ecaf", left, coupler, preferred_element_type=jnp.float32)


def right_plain(left, coupler):
    return jnp.einsum("ecad,df->ecaf", left, coupler, preferred_element_type=jnp.float32)


def per_device(lesser, greater, coulomb_diag, coulomb_upper):
    greater_t = jnp.swapaxes(greater, 3, 4)
    lesser_x, greater_x = (
        lax.all_to_all(lesser, "energy", split_axis=3, concat_axis=0, tiled=True),
        lax.all_to_all(greater_t, "energy", split_axis=3, concat_axis=0, tiled=True),
    )
    polar_x = correlate(lesser_x, greater_x)
    polar = lax.all_to_all(polar_x, "energy", split_axis=0, concat_axis=3, tiled=True)
    own = polar[:, 0]
    diag_block = coulomb_diag[0]
    upper_block = coulomb_upper[0]
    total = right_transposed(left_plain(diag_block, own), diag_block)
    polar_next = from_behind(polar, "space", -1)
    outgoing = right_plain(left_transposed(upper_block, own), upper_block)
    total = total + right_transposed(left_plain(upper_block, polar_next[:, 0]), upper_block)
    incoming = from_behind(outgoing.astype(jnp.bfloat16), "space", 1).astype(outgoing.dtype)
    total = total + incoming
    return total.astype(jnp.bfloat16)[:, None]


def solution(mesh):
    placed = (
        P("energy", "space", None, None, None),
        P("energy", "space", None, None, None),
        P("space", None, None),
        P("space", None, None),
    )
    return jax.shard_map(
        per_device,
        mesh=mesh,
        in_specs=placed,
        out_specs=P("energy", "space", None, None, None),
        check_vma=False,
    )
```

profile of v0, /device:TPU:0, one launch (start us, length us, event | category | flops | bytes accessed | tf_op | source)
XLA Modules:
  0.0 81.9 jit_solution(16510284216522427563)
XLA Ops:
  0.0 2.0 %copy.27 = bf16[2,1,2,256,256]{3,2,0,1,4:T(2,128)(2,1)} copy(bf16[2,1,2,256,256]{4,3,2,1,0:T(8,128)(2,1)} %param.5) | data formatting | bytes 1048576 | tf_op args[1]
  2.0 8.5 %all-to-all-start.1 = ((bf16[2,1,2,256,256]{4,2,0,1,3:T(2,128)(2,1)}), bf16[2,1,2,256,256]{4,2,0,1,3:T(2,128)(2,1)S(1)}, u32[]{:S(2)}, u32[]{:S(2)}) async-start(bf16[2,1,2,256,256]{4,2,0,1,3:T(2,128)(2,1)} %bitcast.3), calls=%async_computation.1 | async-start | bytes 1048576 | tf_op jit(solution)/shard_map/all_to_all | solution.py:91
  10.5 1.3 %copy.24 = bf16[2,1,2,256,256]{4,2,0,1,3:T(2,128)(2,1)} copy(bf16[2,1,2,256,256]{4,3,2,1,0:T(8,128)(2,1)S(1)} %copy-done.4) | data formatting | bytes 1048576 | tf_op args[0]
  11.9 13.7 %all-to-all-done.1 = bf16[2,1,2,256,256]{4,2,0,1,3:T(2,128)(2,1)S(1)} async-done(((bf16[2,1,2,256,256]{4,2,0,1,3:T(2,128)(2,1)}), bf16[2,1,2,256,256]{4,2,0,1,3:T(2,128)(2,1)S(1)}, u32[]{:S(2)}, u32[]{:S(2)}) %all-to-all-start.1) | async-done | bytes 524320 | tf_op jit(solution)/shard_map/all_to_all | solution.py:91
  25.6 3.9 %all-to-all-start = ((bf16[2,1,2,256,256]{4,2,0,1,3:T(2,128)(2,1)}), bf16[2,1,2,256,256]{4,2,0,1,3:T(2,128)(2,1)S(1)}, u32[]{:S(2)}, u32[]{:S(2)}) async-start(bf16[2,1,2,256,256]{4,2,0,1,3:T(2,128)(2,1)} %copy.24), calls=%async_computation | async-start | bytes 1048576 | tf_op jit(solution)/shard_map/all_to_all | solution.py:90
  30.3 1.4 %fusion.48 = f32[64,4096]{1,0:T(8,128)} fusion(bf16[32,4096]{1,0:T(8,128)(2,1)S(1)} %bitcast.110), kind=kOutput, calls=%fused_computation.76 | convolution fusion | flops 16807936 | bytes 1310720 | tf_op jit(solution)/shard_map/dot_general | solution.py:21
  31.7 1.4 %fusion.52 = f32[64,4096]{1,0:T(8,128)} fusion(bf16[32,4096]{1,0:T(8,128)(2,1)S(1)} %bitcast.105), kind=kOutput, calls=%fused_computation.78 | convolution fusion | flops 16807936 | bytes 1310720 | tf_op jit(solution)/shard_map/dot_general | solution.py:21
  33.5 10.5 %all-to-all-done = bf16[2,1,2,256,256]{4,2,0,1,3:T(2,128)(2,1)S(1)} async-done(((bf16[2,1,2,256,256]{4,2,0,1,3:T(2,128)(2,1)}), bf16[2,1,2,256,256]{4,2,0,1,3:T(2,128)(2,1)S(1)}, u32[]{:S(2)}, u32[]{:S(2)}) %all-to-all-start) | async-done | bytes 524320 | tf_op jit(solution)/shard_map/all_to_all | solution.py:90
  45.9 0.4 copy-done.2
  46.4 0.4 convolution_add_fusion.5
  46.8 0.4 convolution_add_fusion.7
  47.2 0.8 copy-done.1
  48.0 0.4 convolution_add_fusion.1
  48.4 0.4 convolution_add_fusion.3
  48.8 0.4 fusion.2
  49.7 0.4 fusion
  50.1 0.6 multiply_add_fusion
  54.4 18.1 %all_to_all.54 = bf16[32,1,2,16,256]{4,3,2,1,0:T(8,128)(2,1)S(1)} all-to-all(bf16[32,1,2,16,256]{4,3,2,1,0:T(8,128)(2,1)S(1)} %pad_maximum_fusion), channel_id=1, replica_groups=mesh['energy'=16,'space'=2] {'energy'}, dimensions={0} | all-to-all | bytes 1048576 | tf_op jit(solution)/shard_map/all_to_all | solution.py:94
  72.7 1.3 %collective-permute-start = (bf16[2,1,2,256,256]{3,4,2,0,1:T(8,128)(2,1)S(1)}, bf16[2,1,2,256,256]{3,4,2,0,1:T(8,128)(2,1)S(1)}, u32[]{:S(2)}, u32[]{:S(2)}) collective-permute-start(bf16[2,1,2,256,256]{3,4,2,0,1:T(8,128)(2,1)S(1)} %copy.36), channel_id=1, source_target_pairs={{1,0},{3,2},{5,4},{7,6},{9,8},{11,10},{13,12},{15,14},{17,16},{19,... | collective-permute-start | bytes 1572872 | tf_op jit(solution)/shard_map/ppermute | solution.py:11
  74.0 1.6 %convolution_convert_fusion = bf16[2,2,256,256]{3,2,1,0:T(8,128)(2,1)} fusion(bf16[2,2,256,256]{3,2,1,0:T(8,128)(2,1)S(1)} %bitcast.122, bf16[1,256,256]{2,1,0:T(8,128)(2,1)S(1)} %copy-done), kind=kOutput, calls=%fused_computation.29 | convolution fusion | flops 268959744 | bytes 1179648 | tf_op jit(solution)/shard_map/ecad,df->ecaf/dot_general | solution.py:84
  75.6 3.1 %collective-permute-start.1 = (bf16[2,2,256,256]{3,2,1,0:T(8,128)(2,1)}, bf16[2,2,256,256]{3,2,1,0:T(8,128)(2,1)S(1)}, u32[]{:S(2)}, u32[]{:S(2)}) collective-permute-start(bf16[2,2,256,256]{3,2,1,0:T(8,128)(2,1)} %convolution_convert_fusion), channel_id=1, source_target_pairs={{0,1},{2,3},{4,5},{6,7},{8,9},{10,11},{12,13},{14,15},{16,17},{18,... | collective-permute-start | bytes 1572872 | tf_op jit(solution)/shard_map/ppermute | solution.py:11
  78.7 0.7 fusion.13
  79.4 1.0 %collective-permute-done.1 = bf16[2,2,256,256]{3,2,1,0:T(8,128)(2,1)S(1)} collective-permute-done((bf16[2,2,256,256]{3,2,1,0:T(8,128)(2,1)}, bf16[2,2,256,256]{3,2,1,0:T(8,128)(2,1)S(1)}, u32[]{:S(2)}, u32[]{:S(2)}) %collective-permute-start.1) | collective-permute-done | bytes 524320 | tf_op jit(solution)/shard_map/ppermute | solution.py:11
  80.4 1.5 %fusion.18 = bf16[2,1,2,256,256]{4,3,2,1,0:T(8,128)(2,1)} fusion(f32[2,2,256,256]{3,2,1,0:T(8,128)S(1)} %fusion.13, bf16[2,2,256,256]{3,2,1,0:T(8,128)(2,1)S(1)} %collective-permute-done.1, bf16[2,1,2,256,256]{3,4,2,0,1:T(8,128)(2,1)S(1)} %collective-permute-done, bf16[1,256,256]{2,1,0:T(8,128)(2,1)S(1)} %copy-done), kind=kOutput, calls=%fused_computation.39 | convolution fusion | flops 269746176 | bytes 2752512 | tf_op jit(solution)/shard_map/ecad,fd->ecaf/dot_general | solution.py:80
  (43 shorter events, 7.3 us)
Async XLA Ops:
  0.0 74.0 %copy-start = (bf16[1,256,256]{2,1,0:T(8,128)(2,1)S(1)}, bf16[1,256,256]{2,1,0:T(8,128)(2,1)}, u32[]{:S(2)}) copy-start(bf16[1,256,256]{2,1,0:T(8,128)(2,1)} %param.7) | copy-start | bytes 393220
  2.0 8.5 %copy-start.4 = (bf16[2,1,2,256,256]{4,3,2,1,0:T(8,128)(2,1)S(1)}, bf16[2,1,2,256,256]{4,3,2,1,0:T(8,128)(2,1)}, u32[]{:S(2)}) copy-start(bf16[2,1,2,256,256]{4,3,2,1,0:T(8,128)(2,1)} %param.4) | copy-start | bytes 1572868
  2.0 23.6 %all-to-all-start.1 = ((bf16[2,1,2,256,256]{4,2,0,1,3:T(2,128)(2,1)}), bf16[2,1,2,256,256]{4,2,0,1,3:T(2,128)(2,1)S(1)}, u32[]{:S(2)}, u32[]{:S(2)}) async-start(bf16[2,1,2,256,256]{4,2,0,1,3:T(2,128)(2,1)} %bitcast.3), calls=%async_computation.1 | async-start | bytes 1048576 | tf_op jit(solution)/shard_map/all_to_all | solution.py:91
  25.6 18.4 %all-to-all-start = ((bf16[2,1,2,256,256]{4,2,0,1,3:T(2,128)(2,1)}), bf16[2,1,2,256,256]{4,2,0,1,3:T(2,128)(2,1)S(1)}, u32[]{:S(2)}, u32[]{:S(2)}) async-start(bf16[2,1,2,256,256]{4,2,0,1,3:T(2,128)(2,1)} %copy.24), calls=%async_computation | async-start | bytes 1048576 | tf_op jit(solution)/shard_map/all_to_all | solution.py:90
  45.1 1.2 %copy-start.2 = (f32[64,4096]{1,0:T(8,128)S(1)}, f32[64,4096]{1,0:T(8,128)}, u32[]{:S(2)}) copy-start(f32[64,4096]{1,0:T(8,128)} %fusion.52) | copy-start | bytes 3145732
  46.8 1.2 %copy-start.1 = (f32[64,4096]{1,0:T(8,128)S(1)}, f32[64,4096]{1,0:T(8,128)}, u32[]{:S(2)}) copy-start(f32[64,4096]{1,0:T(8,128)} %fusion.48) | copy-start | bytes 3145732
  72.7 6.7 %collective-permute-start = (bf16[2,1,2,256,256]{3,4,2,0,1:T(8,128)(2,1)S(1)}, bf16[2,1,2,256,256]{3,4,2,0,1:T(8,128)(2,1)S(1)}, u32[]{:S(2)}, u32[]{:S(2)}) collective-permute-start(bf16[2,1,2,256,256]{3,4,2,0,1:T(8,128)(2,1)S(1)} %copy.36), channel_id=1, source_target_pairs={{1,0},{3,2},{5,4},{7,6},{9,8},{11,10},{13,12},{15,14},{17,16},{19,... | collective-permute-start | bytes 1572872 | tf_op jit(solution)/shard_map/ppermute | solution.py:11
  74.0 4.7 %copy-start.3 = (bf16[1,256,256]{2,1,0:T(8,128)(2,1)S(1)}, bf16[1,256,256]{2,1,0:T(8,128)(2,1)}, u32[]{:S(2)}) copy-start(bf16[1,256,256]{2,1,0:T(8,128)(2,1)} %param.6) | copy-start | bytes 393220
  75.6 4.8 %collective-permute-start.1 = (bf16[2,2,256,256]{3,2,1,0:T(8,128)(2,1)}, bf16[2,2,256,256]{3,2,1,0:T(8,128)(2,1)S(1)}, u32[]{:S(2)}, u32[]{:S(2)}) collective-permute-start(bf16[2,2,256,256]{3,2,1,0:T(8,128)(2,1)} %convolution_convert_fusion), channel_id=1, source_target_pairs={{0,1},{2,3},{4,5},{6,7},{8,9},{10,11},{12,13},{14,15},{16,17},{18,... | collective-permute-start | bytes 1572872 | tf_op jit(solution)/shard_map/ppermute | solution.py:11
where the time goes:
time: 82.4 us; the launch traced here: 81.9 us
  waiting for transfers between devices  25.2 us (31%)
  blocking collectives  18.1 us (22%)
  starting transfers between devices  16.8 us (20%)
  matrix products  15.8 us (19%)
  local copies, waits for them, and re-layouts  5.65 us (7%)
    all_to_all x1, blocking collectives, per_device(): lax.all_to_all(polar_x, 'energy', split_axis=0, concat_axis=3, tiled=True)  18.1 us
    all_to_all x1, waiting for transfers between devices, per_device(): lax.all_to_all(greater_t, 'energy', split_axis=3, concat_axis=0, tiled=True)  13.7 us
    all_to_all x1, waiting for transfers between devices, per_device(): lax.all_to_all(lesser, 'energy', split_axis=3, concat_axis=0, tiled=True)  10.5 us
    all_to_all x1, starting transfers between devices, per_device(): lax.all_to_all(greater_t, 'energy', split_axis=3, concat_axis=0, tiled=True)  8.47 us
    dot_general x8, matrix products, product_two(): jnp.dot(table[0], data_bf, preferred_element_type=jnp.float32)  5.1 us
    unnamed x18, local copies, waits for them, and re-layouts  5.07 us
    ppermute x2, starting transfers between devices, from_behind(): lax.ppermute(value, axis, [(source, source + steps) for source in range(l...  4.37 us
    all_to_all x1, starting transfers between devices, per_device(): lax.all_to_all(lesser, 'energy', split_axis=3, concat_axis=0, tiled=True)  3.95 us
  transfers between devices with their start and end apart: 4, of which 3 were waited for; matrix products, arithmetic and copies ran while one was open for 9% of the time, Pallas kernels for 0%

commit v1 on v0

--- a/solution.py
+++ b/solution.py
@@ -3,6 +3,13 @@
 import jax.numpy as jnp
 from jax import lax
 from jax.sharding import PartitionSpec as P
+
+
+def exchange_blocks(shard, mesh_axis, split, join):
+    devices = lax.axis_size(mesh_axis)
+    blocks = jnp.stack(jnp.split(shard, devices, axis=split), axis=0)
+    blocks = lax.all_to_all(blocks, mesh_axis, split_axis=0, concat_axis=0)
+    return jnp.concatenate(blocks, axis=join)
 
 
 def from_behind(value, axis, steps):
@@ -88,7 +95,7 @@
     greater_t = jnp.swapaxes(greater, 3, 4)
     lesser_x, greater_x = (
         lax.all_to_all(lesser, "energy", split_axis=3, concat_axis=0, tiled=True),
-        lax.all_to_all(greater_t, "energy", split_axis=3, concat_axis=0, tiled=True),
+        exchange_blocks(greater_t, "energy", 3, 0),
     )
     polar_x = correlate(lesser_x, greater_x)
     polar = lax.all_to_all(polar_x, "energy", split_axis=0, concat_axis=3, tiled=True)

time: 82.4 us -> 91.5 us (1.11)
  local copies, waits for them, and re-layouts: 5.65 us -> 14.6 us
    unnamed x18 -> x33, local copies, waits for them, and re-layouts: 5.07 us -> 13.6 us
  transfers between devices with their start and end apart: 4 -> 4, of which waited for: 3 -> 3; matrix products, arithmetic and copies ran while one was open for 9% -> 8% of each run, Pallas kernels for 0% -> 0%
where the time goes in v1:
time: 91.5 us; the launch traced here: 91 us
  waiting for transfers between devices  25.3 us (28%)
  blocking collectives  18.1 us (20%)
  starting transfers between devices  16.8 us (18%)
  matrix products  15.8 us (17%)
  local copies, waits for them, and re-layouts  14.6 us (16%)
    all_to_all x1, blocking collectives, per_device(): lax.all_to_all(polar_x, 'energy', split_axis=0, concat_axis=3, tiled=True)  18.1 us
    all_to_all x1, waiting for transfers between devices, exchange_blocks(): blocks = lax.all_to_all(blocks, mesh_axis, split_axis=0, concat_axis=0)  13.7 us
    unnamed x33, local copies, waits for them, and re-layouts  13.6 us
    all_to_all x1, waiting for transfers between devices, per_device(): lax.all_to_all(lesser, 'energy', split_axis=3, concat_axis=0, tiled=True)  10.6 us
    all_to_all x1, starting transfers between devices, exchange_blocks(): blocks = lax.all_to_all(blocks, mesh_axis, split_axis=0, concat_axis=0)  8.47 us
    dot_general x8, matrix products, product_two(): jnp.dot(table[0], data_bf, preferred_element_type=jnp.float32)  5.1 us
    ppermute x2, starting transfers between devices, from_behind(): lax.ppermute(value, axis, [(source, source + steps) for source in range(l...  4.37 us
    all_to_all x1, starting transfers between devices, per_device(): lax.all_to_all(lesser, 'energy', split_axis=3, concat_axis=0, tiled=True)  3.95 us
  transfers between devices with their start and end apart: 4, of which 3 were waited for; matrix products, arithmetic and copies ran while one was open for 8% of the time, Pallas kernels for 0%

profile of v1, /device:TPU:0, one launch (start us, length us, event | category | flops | bytes accessed | tf_op | source)
XLA Modules:
  0.0 91.0 jit_solution(9685016011702220772)
XLA Ops:
  0.0 1.3 %copy.72 = bf16[2,1,2,256,256]{3,4,2,0,1:T(8,128)(2,1)S(1)} copy(bf16[2,1,2,256,256]{4,3,2,1,0:T(8,128)(2,1)} %param.5) | data formatting | bytes 1048576 | tf_op args[1]
  1.3 0.6 constant_dynamic-update-slice_fusion.15
  1.9 0.6 constant_dynamic-update-slice_fusion.14
  2.5 0.6 constant_dynamic-update-slice_fusion.13
  3.1 0.6 constant_dynamic-update-slice_fusion.12
  3.8 0.6 constant_dynamic-update-slice_fusion.11
  4.4 0.6 constant_dynamic-update-slice_fusion.10
  7.5 0.6 constant_dynamic-update-slice_fusion.5
  11.2 8.5 %all-to-all-start.1 = ((bf16[16,2,1,2,16,256]{5,4,3,2,1,0:T(8,128)(2,1)}), bf16[16,2,1,2,16,256]{5,4,3,2,1,0:T(8,128)(2,1)S(1)}, u32[]{:S(2)}, u32[]{:S(2)}) async-start(bf16[16,2,1,2,16,256]{5,4,3,2,1,0:T(8,128)(2,1)} %constant_dynamic-update-slice_fusion), calls=%async_computation.1 | async-start | bytes 1048576 | tf_op jit(solution)/shard_map/all_to_all | solution.py:11
  19.7 1.3 %copy.69 = bf16[2,1,2,256,256]{4,2,0,1,3:T(2,128)(2,1)} copy(bf16[2,1,2,256,256]{4,3,2,1,0:T(8,128)(2,1)S(1)} %copy-done.4) | data formatting | bytes 1048576 | tf_op args[0]
  21.0 13.7 %all-to-all-done.1 = bf16[16,2,1,2,16,256]{5,4,3,2,1,0:T(8,128)(2,1)S(1)} async-done(((bf16[16,2,1,2,16,256]{5,4,3,2,1,0:T(8,128)(2,1)}), bf16[16,2,1,2,16,256]{5,4,3,2,1,0:T(8,128)(2,1)S(1)}, u32[]{:S(2)}, u32[]{:S(2)}) %all-to-all-start.1) | async-done | bytes 524320 | tf_op jit(solution)/shard_map/all_to_all | solution.py:11
  34.7 3.9 %all-to-all-start = ((bf16[2,1,2,256,256]{4,2,0,1,3:T(2,128)(2,1)}), bf16[2,1,2,256,256]{4,2,0,1,3:T(2,128)(2,1)S(1)}, u32[]{:S(2)}, u32[]{:S(2)}) async-start(bf16[2,1,2,256,256]{4,2,0,1,3:T(2,128)(2,1)} %copy.69), calls=%async_computation | async-start | bytes 1048576 | tf_op jit(solution)/shard_map/all_to_all | solution.py:97
  39.3 1.4 %fusion.48 = f32[64,4096]{1,0:T(8,128)} fusion(bf16[32,4096]{1,0:T(8,128)(2,1)S(1)} %bitcast.203), kind=kOutput, calls=%fused_computation.108 | convolution fusion | flops 16807936 | bytes 1310720 | tf_op jit(solution)/shard_map/dot_general | solution.py:28
  40.7 1.4 %fusion.52 = f32[64,4096]{1,0:T(8,128)} fusion(bf16[32,4096]{1,0:T(8,128)(2,1)S(1)} %bitcast.198), kind=kOutput, calls=%fused_computation.110 | convolution fusion | flops 16807936 | bytes 1310720 | tf_op jit(solution)/shard_map/dot_general | solution.py:28
  42.5 10.6 %all-to-all-done = bf16[2,1,2,256,256]{4,2,0,1,3:T(2,128)(2,1)S(1)} async-done(((bf16[2,1,2,256,256]{4,2,0,1,3:T(2,128)(2,1)}), bf16[2,1,2,256,256]{4,2,0,1,3:T(2,128)(2,1)S(1)}, u32[]{:S(2)}, u32[]{:S(2)}) %all-to-all-start) | async-done | bytes 524320 | tf_op jit(solution)/shard_map/all_to_all | solution.py:97
  55.9 0.8 copy-done.1
  59.2 0.6 multiply_add_fusion
  63.5 18.1 %all_to_all.41 = bf16[32,1,2,16,256]{4,3,2,1,0:T(8,128)(2,1)S(1)} all-to-all(bf16[32,1,2,16,256]{4,3,2,1,0:T(8,128)(2,1)S(1)} %pad_maximum_fusion), channel_id=1, replica_groups=mesh['energy'=16,'space'=2] {'energy'}, dimensions={0} | all-to-all | bytes 1048576 | tf_op jit(solution)/shard_map/all_to_all | solution.py:101
  81.9 1.3 %collective-permute-start = (bf16[2,1,2,256,256]{3,4,2,0,1:T(8,128)(2,1)S(1)}, bf16[2,1,2,256,256]{3,4,2,0,1:T(8,128)(2,1)S(1)}, u32[]{:S(2)}, u32[]{:S(2)}) collective-permute-start(bf16[2,1,2,256,256]{3,4,2,0,1:T(8,128)(2,1)S(1)} %copy.96), channel_id=1, source_target_pairs={{1,0},{3,2},{5,4},{7,6},{9,8},{11,10},{13,12},{15,14},{17,16},{19,... | collective-permute-start | bytes 1572872 | tf_op jit(solution)/shard_map/ppermute | solution.py:18
  83.2 1.6 %convolution_convert_fusion = bf16[2,2,256,256]{3,2,1,0:T(8,128)(2,1)} fusion(bf16[2,2,256,256]{3,2,1,0:T(8,128)(2,1)S(1)} %bitcast.215, bf16[1,256,256]{2,1,0:T(8,128)(2,1)S(1)} %copy-done), kind=kOutput, calls=%fused_computation.29 | convolution fusion | flops 268959744 | bytes 1179648 | tf_op jit(solution)/shard_map/ecad,df->ecaf/dot_general | solution.py:91
  84.7 3.1 %collective-permute-start.1 = (bf16[2,2,256,256]{3,2,1,0:T(8,128)(2,1)}, bf16[2,2,256,256]{3,2,1,0:T(8,128)(2,1)S(1)}, u32[]{:S(2)}, u32[]{:S(2)}) collective-permute-start(bf16[2,2,256,256]{3,2,1,0:T(8,128)(2,1)} %convolution_convert_fusion), channel_id=1, source_target_pairs={{0,1},{2,3},{4,5},{6,7},{8,9},{10,11},{12,13},{14,15},{16,17},{18,... | collective-permute-start | bytes 1572872 | tf_op jit(solution)/shard_map/ppermute | solution.py:18
  87.8 0.7 fusion.13
  88.6 1.0 %collective-permute-done.1 = bf16[2,2,256,256]{3,2,1,0:T(8,128)(2,1)S(1)} collective-permute-done((bf16[2,2,256,256]{3,2,1,0:T(8,128)(2,1)}, bf16[2,2,256,256]{3,2,1,0:T(8,128)(2,1)S(1)}, u32[]{:S(2)}, u32[]{:S(2)}) %collective-permute-start.1) | collective-permute-done | bytes 524320 | tf_op jit(solution)/shard_map/ppermute | solution.py:18
  89.5 1.5 %fusion.18 = bf16[2,1,2,256,256]{4,3,2,1,0:T(8,128)(2,1)} fusion(f32[2,2,256,256]{3,2,1,0:T(8,128)S(1)} %fusion.13, bf16[2,2,256,256]{3,2,1,0:T(8,128)(2,1)S(1)} %collective-permute-done.1, bf16[2,1,2,256,256]{3,4,2,0,1:T(8,128)(2,1)S(1)} %collective-permute-done, bf16[1,256,256]{2,1,0:T(8,128)(2,1)S(1)} %copy-done), kind=kOutput, calls=%fused_computation.39 | convolution fusion | flops 269746176 | bytes 2752512 | tf_op jit(solution)/shard_map/ecad,fd->ecaf/dot_general | solution.py:87
  (57 shorter events, 15.6 us)
Async XLA Ops:
  0.0 83.2 %copy-start = (bf16[1,256,256]{2,1,0:T(8,128)(2,1)S(1)}, bf16[1,256,256]{2,1,0:T(8,128)(2,1)}, u32[]{:S(2)}) copy-start(bf16[1,256,256]{2,1,0:T(8,128)(2,1)} %param.7) | copy-start | bytes 393220
  11.2 8.5 %copy-start.4 = (bf16[2,1,2,256,256]{4,3,2,1,0:T(8,128)(2,1)S(1)}, bf16[2,1,2,256,256]{4,3,2,1,0:T(8,128)(2,1)}, u32[]{:S(2)}) copy-start(bf16[2,1,2,256,256]{4,3,2,1,0:T(8,128)(2,1)} %param.4) | copy-start | bytes 1572868
  11.2 23.6 %all-to-all-start.1 = ((bf16[16,2,1,2,16,256]{5,4,3,2,1,0:T(8,128)(2,1)}), bf16[16,2,1,2,16,256]{5,4,3,2,1,0:T(8,128)(2,1)S(1)}, u32[]{:S(2)}, u32[]{:S(2)}) async-start(bf16[16,2,1,2,16,256]{5,4,3,2,1,0:T(8,128)(2,1)} %constant_dynamic-update-slice_fusion), calls=%async_computation.1 | async-start | bytes 1048576 | tf_op jit(solution)/shard_map/all_to_all | solution.py:11
  34.7 18.4 %all-to-all-start = ((bf16[2,1,2,256,256]{4,2,0,1,3:T(2,128)(2,1)}), bf16[2,1,2,256,256]{4,2,0,1,3:T(2,128)(2,1)S(1)}, u32[]{:S(2)}, u32[]{:S(2)}) async-start(bf16[2,1,2,256,256]{4,2,0,1,3:T(2,128)(2,1)} %copy.69), calls=%async_computation | async-start | bytes 1048576 | tf_op jit(solution)/shard_map/all_to_all | solution.py:97
  54.3 1.2 %copy-start.2 = (f32[64,4096]{1,0:T(8,128)S(1)}, f32[64,4096]{1,0:T(8,128)}, u32[]{:S(2)}) copy-start(f32[64,4096]{1,0:T(8,128)} %fusion.52) | copy-start | bytes 3145732
  55.5 1.2 %copy-start.1 = (f32[64,4096]{1,0:T(8,128)S(1)}, f32[64,4096]{1,0:T(8,128)}, u32[]{:S(2)}) copy-start(f32[64,4096]{1,0:T(8,128)} %fusion.48) | copy-start | bytes 3145732
  81.9 6.7 %collective-permute-start = (bf16[2,1,2,256,256]{3,4,2,0,1:T(8,128)(2,1)S(1)}, bf16[2,1,2,256,256]{3,4,2,0,1:T(8,128)(2,1)S(1)}, u32[]{:S(2)}, u32[]{:S(2)}) collective-permute-start(bf16[2,1,2,256,256]{3,4,2,0,1:T(8,128)(2,1)S(1)} %copy.96), channel_id=1, source_target_pairs={{1,0},{3,2},{5,4},{7,6},{9,8},{11,10},{13,12},{15,14},{17,16},{19,... | collective-permute-start | bytes 1572872 | tf_op jit(solution)/shard_map/ppermute | solution.py:18
  83.2 4.7 %copy-start.3 = (bf16[1,256,256]{2,1,0:T(8,128)(2,1)S(1)}, bf16[1,256,256]{2,1,0:T(8,128)(2,1)}, u32[]{:S(2)}) copy-start(bf16[1,256,256]{2,1,0:T(8,128)(2,1)} %param.6) | copy-start | bytes 393220
  84.7 4.8 %collective-permute-start.1 = (bf16[2,2,256,256]{3,2,1,0:T(8,128)(2,1)}, bf16[2,2,256,256]{3,2,1,0:T(8,128)(2,1)S(1)}, u32[]{:S(2)}, u32[]{:S(2)}) collective-permute-start(bf16[2,2,256,256]{3,2,1,0:T(8,128)(2,1)} %convolution_convert_fusion), channel_id=1, source_target_pairs={{0,1},{2,3},{4,5},{6,7},{8,9},{10,11},{12,13},{14,15},{16,17},{18,... | collective-permute-start | bytes 1572872 | tf_op jit(solution)/shard_map/ppermute | solution.py:18
